TPU v7x, 32 devices: a whole 2x2x4 slice. The times are simulated.
32 devices in a mesh: leaf: 32 (over z, y, x, core).
Axes of the slice: x: 2, y: 2, z: 4, core: 2. Of those that a mesh axis runs over, the one named last changes fastest.
Arguments:
- points: float32 [3, 131072], P(None, 'leaf'), may hold values from 0 to 1
- rhs: float32 [16, 131072], P(None, 'leaf'), may hold values from -6 to 6
- leaf_basis: float32 [32, 131072], P(None, 'leaf'), may hold values from -0.75 to 0.75
- transfer: float32 [32, 32, 2688], P(None, None, 'leaf'), may hold values from -0.5 to 0.5
- proxies: float32 [3, 32, 2720], P(None, None, 'leaf'), may hold values from 0 to 1
- near_list: int32 [2048, 5], P('leaf'), may hold values from -1 to 2047, as said below
- couple_list: int32 [2688, 20], P('leaf'), may hold values from -1 to 2047, as said below
- root_list: int32 [32, 32], P('leaf'), may hold values from -1 to 31, as said below
Outputs:
- product: float32 [16, 131072], P(None, 'leaf')
Inputs may be any that keep to these rules, and one draw needn't show every extreme that they name: `near_list`: entry [t, j] is the leaf t + j - 2 if the block of leaves t and t + j - 2 is near, else -1; every leaf is near itself. Nearness is defined level by level: at level 0 roots t and s are near when they differ by at most a per-root reach of 1 to 2 (the larger of the two); below, two clusters are near when their parents are near and they differ by at most the larger of their reaches. Near leaf blocks, with the coupled pairs of the other two lists, cover every pair of points exactly once. `couple_list`: the row of a cluster t of level l lists in slot j the cluster s = 4 * (t // 4 - 2) + j of level l if s exists, the parents of t and s are near and t and s are not near, else -1. `root_list`: entry [t, s] is s if roots t and s are not near, else -1.
All inputs are finite; a program needn't handle non-finite values.
Results may differ from a plain program's by a relative error of at most 0.0003.
Values sent between devices are 32-bit elements; how exact they have to be, the bound alone decides.
No kernel may reach another device: no remote copies, remote signals or barrier semaphores. Data moves between devices by JAX's collectives and lax.ppermute only.
A program may use at most 128 MiB of HBM per device.

v0:
```python
import math
import jax
import jax.numpy as jnp
from jax import lax
from jax.sharding import PartitionSpec as P

LEAF = 64
LEVELS = 3
REACH = 2
HALO = 11
LEAF_DEV = 64
kernel_band = 0.1
highest = lax.Precision.HIGHEST


def with_halo_2(cells, sides, width):
    for axis, dim in sides:
        count = lax.axis_size(axis)
        ends = count - 1
        head = lax.slice_in_dim(cells, 0, width, axis=dim)
        tail = lax.slice_in_dim(cells, cells.shape[dim] - width, cells.shape[dim], axis=dim)
        cells = jnp.concatenate(
            [
                lax.ppermute(tail, axis, [(i, (i + 1) % count) for i in range(ends)]),
                cells,
                lax.ppermute(head, axis, [((i + 1) % count, i) for i in range(ends)]),
            ],
            axis=dim,
        )
    return cells


def kernel_sq(left_pts, right_pts):
    length = (
        (left_pts[0] - right_pts[0]) ** 2
        + (left_pts[1] - right_pts[1]) ** 2
        + (left_pts[2] - right_pts[2]) ** 2
    )
    return jnp.exp(-length / kernel_band)


def by_blocks(method, inputs, length, stride, out_shape):
    stride = math.gcd(length, stride)

    def advance(step_no, accumulated):
        pieces = [operand for operand in inputs]
        return method(*pieces)

    return lax.fori_loop(0, length // stride, advance, jnp.zeros(out_shape, jnp.float32))


def couple(target_prox, lookup, source_prox, listed):
    usable = listed.T >= 0
    clipped = jnp.where(usable, listed.T, 0)

    def one_block(target_blk, clipped_blk, usable_blk):
        coeff_blk = jnp.take(lookup, clipped_blk, axis=2)
        prox_blk = jnp.take(source_prox, clipped_blk, axis=2)
        kernel = kernel_sq(
            target_blk[:, :, None, None, :], prox_blk[:, None, :, :, :]
        ) * usable_blk.astype(coeff_blk.dtype)
        return jnp.einsum("absn,bksn->akn", kernel, coeff_blk, precision=highest)

    extent = listed.shape[0]
    return by_blocks(
        one_block,
        [target_prox, clipped, usable],
        extent,
        128,
        (lookup.shape[0], lookup.shape[1], extent),
    )


def near_local(targets, lookup, listed, vectors):
    leaves = targets.shape[1]
    total = jnp.zeros((vectors, leaves, targets.shape[2]), jnp.float32)
    for slot_no in range(listed.shape[1]):
        window = lookup[:, slot_no : slot_no + leaves]
        usable = (listed[:, slot_no] >= 0).astype(jnp.float32)
        kernel = (
            kernel_sq(targets[:, :, :, None], window[vectors:, :, None, :]) * usable[:, None, None]
        )
        total = total + jnp.einsum("nij,knj->kni", kernel, window[:vectors], precision=highest)
    return total


def body(points, rhs, leaf_basis, transfer, proxies, near_list, couple_list, root_list):
    device = lax.axis_index("leaf")
    rank_dim = leaf_basis.shape[0]
    vectors = rhs.shape[0]
    leaves = LEAF_DEV
    basis_grid = leaf_basis.reshape(rank_dim, leaves, LEAF)
    coeffs = [None] * (LEVELS + 1)
    coeffs[LEVELS] = jnp.einsum(
        "rnp,knp->rkn", basis_grid, rhs.reshape(vectors, leaves, LEAF), precision=highest
    )
    level_prox = []
    mappings = [None]
    entries = [None]
    for level_no in range(LEVELS + 1):
        extent = 4**level_no
        begin_at = (extent - 1) // 3
        level_prox.append(proxies[:, :, begin_at : begin_at + extent])
        if level_no > 0:
            mappings.append(transfer[:, :, begin_at - 1 : begin_at - 1 + extent])
            entries.append(couple_list[begin_at - 1 : begin_at - 1 + extent])
    for level_no in range(LEVELS, 0, -1):
        merged = jnp.einsum("abn,akn->bkn", mappings[level_no], coeffs[level_no], precision=highest)
        coeffs[level_no - 1] = merged.reshape(rank_dim, vectors, -1, 4).sum(axis=3)
    top_count = 3
    stacked_coeffs = jnp.concatenate([coeffs[level_no] for level_no in range(top_count)], axis=2)
    stacked_prox = jnp.concatenate(level_prox[:top_count], axis=2)
    gathered_coeffs, gathered_prox = (
        lax.all_gather(stacked_coeffs, "leaf", axis=2, tiled=True),
        lax.all_gather(stacked_prox, "leaf", axis=2, tiled=True),
    )
    group = stacked_coeffs.shape[2]
    roots = gathered_coeffs.shape[2] // group
    gathered_coeffs = gathered_coeffs.reshape(rank_dim, vectors, roots, group)
    gathered_prox = gathered_prox.reshape(3, rank_dim, roots, group)
    coupled = []
    for level_no in range(LEVELS + 1):
        extent = 4**level_no
        if level_no < top_count:
            begin_at = (extent - 1) // 3
            lookup = gathered_coeffs[:, :, :, begin_at : begin_at + extent].reshape(
                rank_dim, vectors, roots * extent
            )
            source_prox = gathered_prox[:, :, :, begin_at : begin_at + extent].reshape(
                3, rank_dim, roots * extent
            )
            listed = root_list if level_no == 0 else entries[level_no]
        else:
            joined = jnp.concatenate(
                [
                    coeffs[level_no].reshape(rank_dim * vectors, extent),
                    level_prox[level_no].reshape(3 * rank_dim, extent),
                ],
                axis=0,
            )
            with_rim = with_halo_2(joined, (("leaf", 1),), HALO)
            width_rim = with_rim.shape[1]
            lookup = with_rim[: rank_dim * vectors].reshape(rank_dim, vectors, width_rim)
            source_prox = with_rim[rank_dim * vectors :].reshape(3, rank_dim, width_rim)
            base_index = device * extent - HALO
            listed = jnp.where(entries[level_no] >= 0, entries[level_no] - base_index, -1)
        coupled.append(couple(level_prox[level_no], lookup, source_prox, listed))
    downward = coupled[0]
    for level_no in range(1, LEVELS + 1):
        downward = coupled[level_no] + jnp.einsum(
            "abn,bkn->akn", mappings[level_no], jnp.repeat(downward, 4, axis=2), precision=highest
        )
    joined_pts = jnp.concatenate([rhs, points], axis=0)
    with_halo = with_halo_2(joined_pts, (("leaf", 1),), REACH * LEAF)
    lookup_pts = with_halo.reshape(vectors + 3, leaves + 2 * REACH, LEAF)
    targets = points.reshape(3, leaves, LEAF)
    near_part = near_local(targets, lookup_pts, near_list, vectors)
    far_part = jnp.einsum("rnp,rkn->knp", basis_grid, downward, precision=highest)
    return (near_part + far_part).reshape(vectors, leaves * LEAF)


def solution(mesh):
    in_specs = (
        P(None, "leaf"),
        P(None, "leaf"),
        P(None, "leaf"),
        P(None, None, "leaf"),
        P(None, None, "leaf"),
        P("leaf", None),
        P("leaf", None),
        P("leaf", None),
    )
    out_specs = P(None, "leaf")
    return jax.shard_map(body, mesh=mesh, in_specs=in_specs, out_specs=out_specs, check_vma=False)
```

profile of v0, /device:TPU:0, one launch (start us, length us, event | category | flops | bytes accessed | tf_op | source)
XLA Modules:
  0.0 221.3 jit_solution(3418273684707584734)
XLA Ops:
  6.5 1.3 slice.387
  7.9 2.0 slice.388
  10.3 1.2 reshape.363
  12.4 1.7 copy.166
  14.4 3.6 %convolution_bitcast_fusion = f32[32,16,64]{0,1,2:T(8,128)S(1)} fusion(f32[32,64,64]{2,1,0:T(8,128)S(1)} %reshape.364, f32[16,64,64]{2,1,0:T(8,128)} %reshape.363), kind=kOutput, calls=%fused_computation.140 | convolution fusion | flops 25165824 | bytes 917504 | tf_op jit(solution)/shard_map/rnp,knp->rkn/dot_general | solution.py:94
  18.1 1.0 bitcast_reduce_fusion
  21.8 2.4 %collective-permute-start.2 = (f32[608,11]{1,0:T(8,128)}, f32[608,11]{1,0:T(8,128)S(1)}, u32[]{:S(2)}, u32[]{:S(2)}) collective-permute-start(f32[608,11]{1,0:T(8,128)} %get-tuple-element.121), channel_id=1, source_target_pairs={{0,1},{1,2},{2,3},{3,4},{4,5},{5,6},{6,7},{7,8},{8,9},{9,10},{10,1... | collective-permute-start | bytes 80264 | tf_op jit(solution)/shard_map/ppermute | solution.py:24
  24.2 1.3 collective-permute-start.3
  26.2 5.7 %collective-permute-start = (f32[19,128]{1,0:T(8,128)}, f32[19,128]{1,0:T(8,128)}, u32[]{:S(2)}, u32[]{:S(2)}) collective-permute-start(f32[19,128]{1,0:T(8,128)} %get-tuple-element.119), channel_id=1, source_target_pairs={{0,1},{1,2},{2,3},{3,4},{4,5},{5,6},{6,7},{7,8},{8,9},{9,10},{10,1... | collective-permute-start | bytes 29192 | tf_op jit(solution)/shard_map/ppermute | solution.py:24
  31.9 1.3 collective-permute-start.1
  34.7 50.4 %all_gather.7 = f32[3,32,672]{1,0,2:T(4,128)S(1)} all-gather(f32[3,32,21]{1,0,2:T(4,128)S(1)} %copy.169), channel_id=1, replica_groups=mesh['leaf'=32] {'leaf'}, dimensions={2}, use_global_device_ids=true | all-gather | bytes 266112 | tf_op jit(solution)/shard_map/all_gather | solution.py:115
  93.2 2.2 gather_fusion.3
  104.8 6.1 %fusion.87 = f32[64,16,64]{2,1,0:T(8,128)S(1)} fusion(f32[64]{0:T(128)S(1)} %get-tuple-element.145, f32[64,64]{1,0:T(8,128)S(1)} %get-tuple-element.100, f32[64,64]{1,0:T(8,128)S(1)} %get-tuple-element.101, f32[64,64]{1,0:T(8,128)S(1)} %get-tuple-element.102, f32[64,64]{1,0:T(8,128)S(1)} %sub.523, f32[64,64]{1,0:T(8,128)S(1)} %sub.518, ...), kind=kOutput, calls=%fused_computation.95 | convolution fusion | flops 53215232 | bytes 622848 | tf_op jit(solution)/shard_map/nij,knj->kni/dot_general | solution.py:83
  110.9 6.1 %fusion.74 = f32[64,16,64]{2,1,0:T(8,128)S(1)} fusion(f32[64]{0:T(128)S(1)} %get-tuple-element.144, f32[64,64]{1,0:T(8,128)S(1)} %get-tuple-element.89, f32[64,64]{1,0:T(8,128)S(1)} %get-tuple-element.90, f32[64,64]{1,0:T(8,128)S(1)} %get-tuple-element.98, f32[64,64]{1,0:T(8,128)S(1)} %sub.523, f32[64,64]{1,0:T(8,128)S(1)} %sub.518, ...), kind=kOutput, calls=%fused_computation.82 | convolution fusion | flops 53215232 | bytes 622848 | tf_op jit(solution)/shard_map/nij,knj->kni/dot_general | solution.py:83
  117.0 6.1 %fusion.48 = f32[64,16,64]{2,1,0:T(8,128)S(1)} fusion(f32[64]{0:T(128)S(1)} %get-tuple-element.147, f32[64,64]{1,0:T(8,128)S(1)} %get-tuple-element.103, f32[64,64]{1,0:T(8,128)S(1)} %get-tuple-element.99, f32[64,64]{1,0:T(8,128)S(1)} %get-tuple-element.88, f32[64,64]{1,0:T(8,128)S(1)} %sub.523, f32[64,64]{1,0:T(8,128)S(1)} %sub.518, ...), kind=kOutput, calls=%fused_computation.56 | convolution fusion | flops 53215232 | bytes 622848 | tf_op jit(solution)/shard_map/nij,knj->kni/dot_general | solution.py:83
  123.0 6.1 %fusion.138 = f32[64,16,64]{2,1,0:T(8,128)S(1)} fusion(f32[64,16,64]{2,1,0:T(8,128)S(1)} %fusion.74, f32[64,16,64]{2,1,0:T(8,128)S(1)} %fusion.87, f32[64]{0:T(128)S(1)} %get-tuple-element.146, f32[64,64]{1,0:T(8,128)S(1)} %get-tuple-element.104, f32[64,64]{1,0:T(8,128)S(1)} %sub.523, f32[64,64]{1,0:T(8,128)S(1)} %get-tuple-element.112, ...), kind=kOutput, calls=%fused_computation.143 | convolution fusion | flops 53346304 | bytes 1147136 | tf_op jit(solution)/shard_map/nij,knj->kni/dot_general | solution.py:83
  129.1 6.0 %fusion.144 = f32[64,16,64]{2,1,0:T(8,128)} fusion(f32[64,16,64]{2,1,0:T(8,128)S(1)} %fusion.48, f32[64,16,64]{2,1,0:T(8,128)S(1)} %fusion.138, f32[64]{0:T(128)S(1)} %get-tuple-element.143, f32[64,64]{1,0:T(8,128)S(1)} %get-tuple-element.86, f32[64,64]{1,0:T(8,128)S(1)} %get-tuple-element.87, f32[64,64]{1,0:T(8,128)S(1)} %get-tuple-element.85, ...), kind=kOutput, calls=%fused_computation.145 | convolution fusion | flops 53346304 | bytes 1147136 | tf_op jit(solution)/shard_map/nij,knj->kni/dot_general | solution.py:83
  136.1 4.3 %gather_fusion.1 = f32[1280,3,32]{2,1,0:T(4,128)S(1)} fusion(f32[3,32,86]{1,0,2:T(4,128)S(1)} %copy.122, s32[2048]{0:T(1024)S(1)} %pad_clamp_fusion), kind=kCustom, calls=%fused_computation.1 | custom fusion | bytes 988160 | tf_op jit(solution)/shard_map/while/body/eval_jaxpr/jit(_take)/gather | solution.py:58
  140.4 2.6 %copy.154 = f32[20,64,3,32]{1,0,3,2:T(8,128)} copy(f32[20,64,3,32]{3,2,1,0:T(4,128)S(1)} %bitcast.205) | data formatting | bytes 983040 | tf_op jit(solution)/shard_map/while/body/eval_jaxpr/jit(_take)/gather | solution.py:58
  143.0 1.4 select_bitcast_fusion
  144.7 1.1 copy.126
  145.8 1.1 copy.128
  147.7 5.5 %gather_fusion = f32[1280,32,16]{1,2,0:T(8,128)} fusion(f32[32,16,86]{0,1,2:T(8,128)S(1)} %copy.120, s32[2048]{0:T(1024)S(1)} %pad_clamp_fusion), kind=kCustom, calls=%fused_computation | custom fusion | bytes 5248000 | tf_op jit(solution)/shard_map/while/body/eval_jaxpr/jit(_take)/gather | solution.py:57
  153.2 31.3 %fusion.130 = f32[64,16,32]{2,1,0:T(8,128)} fusion(f32[20,64]{1,0:T(8,128)S(1)} %copy-done.44, f32[32,20,64]{0,2,1:T(8,128)S(1)} %copy-done.15, f32[32,64]{0,1:T(8,128)S(1)} %copy-done.39, f32[32,20,64]{0,2,1:T(8,128)S(1)} %copy-done.14, f32[32,64]{0,1:T(8,128)S(1)} %copy-done.38, f32[32,20,64]{0,2,1:T(8,128)S(1)} %copy.124, f32[32,64]{0,1:T(8,128)S(1)} %copy-done.37, ...), kind=kOutput, calls=%fused_computation.141 | convolution fusion | flops 266731520 | bytes 3275008 | tf_op jit(solution)/shard_map/while/body/eval_jaxpr/absn,bksn->akn/dot_general | solution.py:62
  184.5 1.3 slice.465
  186.8 4.6 %slice.460 = f32[32,16,32,16]{0,1,3,2:T(8,128)} slice(f32[32,16,32,21]{0,1,3,2:T(8,128)} %bitcast.208), slice={[0:32], [0:16], [0:32], [5:21]} | slice | bytes 2097152 | tf_op jit(solution)/shard_map/slice | solution.py:126
  192.1 1.4 gather_fusion.6
  193.5 3.0 %gather_fusion.2 = f32[320,32,16]{1,2,0:T(8,128)S(1)} fusion(f32[32,16,512]{0,1,2:T(8,128)} %bitcast.203, s32[1024]{0:T(1024)S(1)} %get-tuple-element.151), kind=kCustom, calls=%fused_computation.2 | custom fusion | bytes 1312000 | tf_op jit(solution)/shard_map/while/body/eval_jaxpr/jit(_take)/gather | solution.py:57
  196.7 3.1 %fusion.153 = f32[4,16,32]{2,1,0:T(8,128)S(1)} fusion(f32[20,4,32,16]{2,3,1,0:T(8,128)S(1)} %bitcast.201, f32[20,4]{1,0:T(8,128)} %get-tuple-element.139, f32[32,20,4]{0,2,1:T(4,128)} %get-tuple-element.124, f32[32,4]{0,1:T(4,128)} %bitcast.234, f32[32,20,4]{0,2,1:T(4,128)} %get-tuple-element.125, f32[32,4]{0,1:T(4,128)} %bitcast.233, ...), kind=kOutput, calls=%fused_computation.150 | convolution fusion | flops 16670720 | bytes 204688 | tf_op jit(solution)/shard_map/while/body/eval_jaxpr/absn,bksn->akn/dot_general | solution.py:62
  201.1 8.3 %fusion.148 = f32[16,16,32]{2,1,0:T(8,128)S(1)} fusion(f32[20,16]{1,0:T(8,128)S(1)} %copy-done.43, f32[32,20,16]{0,2,1:T(8,128)S(1)} %copy-done.25, f32[32,16]{0,1:T(8,128)S(1)} %copy-done.47, f32[32,20,16]{0,2,1:T(8,128)S(1)} %copy-done.26, f32[32,16]{0,1:T(8,128)S(1)} %copy-done.46, f32[32,20,16]{0,2,1:T(8,128)S(1)} %copy-done.24, ...), kind=kOutput, calls=%fused_computation.149 | convolution fusion | flops 66682880 | bytes 818752 | tf_op jit(solution)/shard_map/while/body/eval_jaxpr/absn,bksn->akn/dot_general | solution.py:62
  210.0 1.7 fusion.129
  211.8 1.6 fusion.128
  (202 shorter events, 30.1 us)
Async XLA Ops:
  6.5 178.0 %all-gather.2.cloned.1.call-start = ((), (), s32[]{:S(2)}) async-start(), calls=%async_computation | async-start | bytes 5677056 | tf_op jit(solution)/shard_map/all_gather | solution.py:114
  10.3 7.7 %copy-start = (f32[32,64,64]{2,1,0:T(8,128)}, f32[32,64,64]{2,1,0:T(8,128)S(1)}, u32[]{:S(2)}) copy-start(f32[32,64,64]{2,1,0:T(8,128)S(1)} %reshape.364) | copy-start | bytes 1572868
  12.4 6.7 %copy-start.2 = (f32[32,32,64]{1,0,2:T(8,128)}, f32[32,32,64]{1,0,2:T(8,128)S(1)}, u32[]{:S(2)}) copy-start(f32[32,32,64]{1,0,2:T(8,128)S(1)} %copy.165) | copy-start | bytes 786436
  14.4 5.1 %copy-start.16 = (f32[32,32,4]{1,0,2:T(8,128)}, f32[32,32,4]{1,0,2:T(8,128)S(1)}, u32[]{:S(2)}) copy-start(f32[32,32,4]{1,0,2:T(8,128)S(1)} %copy.167) | copy-start | bytes 49156
  19.1 6.4 %copy-start.11 = (f32[16,4096]{1,0:T(8,128)S(1)}, f32[16,4096]{1,0:T(8,128)}, u32[]{:S(2)}) copy-start(f32[16,4096]{1,0:T(8,128)} %param.9) | copy-start | bytes 786436
  19.1 6.4 %copy-start.23 = (f32[3,4096]{1,0:T(4,128)S(1)}, f32[3,4096]{1,0:T(4,128)}, u32[]{:S(2)}) copy-start(f32[3,4096]{1,0:T(4,128)} %param.8) | copy-start | bytes 147460
  19.1 14.1 %copy-start.21 = (s32[84,20]{0,1:T(8,128)S(1)}, s32[84,20]{0,1:T(8,128)}, u32[]{:S(2)}) copy-start(s32[84,20]{0,1:T(8,128)} %param.14) | copy-start | bytes 20164
  20.8 64.3 %copy-start.55 = (s32[1,32]{1,0:T(1,128)S(1)}, s32[1,32]{1,0:T(1,128)}, u32[]{:S(2)}) copy-start(s32[1,32]{1,0:T(1,128)} %param.15) | copy-start | bytes 388
  20.9 114.2 %copy-start.12 = (f32[3,32,64]{2,1,0:T(8,128)}, f32[3,32,64]{2,1,0:T(8,128)S(1)}, u32[]{:S(2)}) copy-start(f32[3,32,64]{2,1,0:T(8,128)S(1)} %slice.375) | copy-start | bytes 73732
  21.8 113.3 %collective-permute-start.2 = (f32[608,11]{1,0:T(8,128)}, f32[608,11]{1,0:T(8,128)S(1)}, u32[]{:S(2)}, u32[]{:S(2)}) collective-permute-start(f32[608,11]{1,0:T(8,128)} %get-tuple-element.121), channel_id=1, source_target_pairs={{0,1},{1,2},{2,3},{3,4},{4,5},{5,6},{6,7},{7,8},{8,9},{9,10},{10,1... | collective-permute-start | bytes 80264 | tf_op jit(solution)/shard_map/ppermute | solution.py:24
  24.2 110.9 %collective-permute-start.3 = (f32[608,11]{1,0:T(8,128)}, f32[608,11]{1,0:T(8,128)S(1)}, u32[]{:S(2)}, u32[]{:S(2)}) collective-permute-start(f32[608,11]{1,0:T(8,128)} %get-tuple-element.122), channel_id=1, source_target_pairs={{1,0},{2,1},{3,2},{4,3},{5,4},{6,5},{7,6},{8,7},{9,8},{10,9},{11,1... | collective-permute-start | bytes 80264 | tf_op jit(solution)/shard_map/ppermute | solution.py:26
  26.2 77.3 %collective-permute-start = (f32[19,128]{1,0:T(8,128)}, f32[19,128]{1,0:T(8,128)}, u32[]{:S(2)}, u32[]{:S(2)}) collective-permute-start(f32[19,128]{1,0:T(8,128)} %get-tuple-element.119), channel_id=1, source_target_pairs={{0,1},{1,2},{2,3},{3,4},{4,5},{5,6},{6,7},{7,8},{8,9},{9,10},{10,1... | collective-permute-start | bytes 29192 | tf_op jit(solution)/shard_map/ppermute | solution.py:24
  31.9 71.6 %collective-permute-start.1 = (f32[19,128]{1,0:T(8,128)}, f32[19,128]{1,0:T(8,128)}, u32[]{:S(2)}, u32[]{:S(2)}) collective-permute-start(f32[19,128]{1,0:T(8,128)} %get-tuple-element.120), channel_id=1, source_target_pairs={{1,0},{2,1},{3,2},{4,3},{5,4},{6,5},{7,6},{8,7},{9,8},{10,9},{11,1... | collective-permute-start | bytes 29192 | tf_op jit(solution)/shard_map/ppermute | solution.py:26
  85.7 6.2 %copy-start.50 = (pred[32]{0:T(512)(128)(4,1)}, pred[32]{0:T(512)(128)(4,1)S(1)}, u32[]{:S(2)}) copy-start(pred[32]{0:T(512)(128)(4,1)S(1)} %get-tuple-element.148) | copy-start | bytes 100
  95.5 4.4 %copy-start.35 = (f32[32,16]{1,0:T(8,128)S(1)}, f32[32,16]{1,0:T(8,128)}, u32[]{:S(2)}) copy-start(f32[32,16]{1,0:T(8,128)} %get-tuple-element.134) | copy-start | bytes 6148
  95.5 5.1 %copy-start.34 = (f32[32,16]{1,0:T(8,128)S(1)}, f32[32,16]{1,0:T(8,128)}, u32[]{:S(2)}) copy-start(f32[32,16]{1,0:T(8,128)} %get-tuple-element.133) | copy-start | bytes 6148
  95.5 5.7 %copy-start.30 = (f32[32,64]{1,0:T(8,128)S(1)}, f32[32,64]{1,0:T(8,128)}, u32[]{:S(2)}) copy-start(f32[32,64]{1,0:T(8,128)} %get-tuple-element.135) | copy-start | bytes 24580
  95.5 6.4 %copy-start.29 = (f32[32,64]{1,0:T(8,128)S(1)}, f32[32,64]{1,0:T(8,128)}, u32[]{:S(2)}) copy-start(f32[32,64]{1,0:T(8,128)} %get-tuple-element.137) | copy-start | bytes 24580
  95.5 7.1 %copy-start.28 = (f32[32,64]{1,0:T(8,128)S(1)}, f32[32,64]{1,0:T(8,128)}, u32[]{:S(2)}) copy-start(f32[32,64]{1,0:T(8,128)} %get-tuple-element.136) | copy-start | bytes 24580
  95.5 7.8 %copy-start.27 = (f32[4096]{0:T(1024)S(1)}, f32[4096]{0:T(1024)}, u32[]{:S(2)}) copy-start(f32[4096]{0:T(1024)} %get-tuple-element.48) | copy-start | bytes 49156
  147.6 5.6 %copy-start.14 = (f32[32,20,64]{0,2,1:T(8,128)S(1)}, f32[32,20,64]{0,2,1:T(8,128)}, u32[]{:S(2)}) copy-start(f32[32,20,64]{0,2,1:T(8,128)} %copy.126) | copy-start | bytes 491524
  147.6 5.6 %copy-start.15 = (f32[32,20,64]{0,2,1:T(8,128)S(1)}, f32[32,20,64]{0,2,1:T(8,128)}, u32[]{:S(2)}) copy-start(f32[32,20,64]{0,2,1:T(8,128)} %copy.128) | copy-start | bytes 491524
  147.6 5.6 %copy-start.37 = (f32[32,64]{0,1:T(8,128)S(1)}, f32[32,64]{0,1:T(8,128)}, u32[]{:S(2)}) copy-start(f32[32,64]{0,1:T(8,128)} %copy.121) | copy-start | bytes 24580
  147.6 5.6 %copy-start.38 = (f32[32,64]{0,1:T(8,128)S(1)}, f32[32,64]{0,1:T(8,128)}, u32[]{:S(2)}) copy-start(f32[32,64]{0,1:T(8,128)} %copy.125) | copy-start | bytes 24580
  147.7 5.6 %copy-start.39 = (f32[32,64]{0,1:T(8,128)S(1)}, f32[32,64]{0,1:T(8,128)}, u32[]{:S(2)}) copy-start(f32[32,64]{0,1:T(8,128)} %copy.127) | copy-start | bytes 24580
  147.7 5.6 %copy-start.44 = (f32[20,64]{1,0:T(8,128)S(1)}, f32[20,64]{1,0:T(8,128)}, u32[]{:S(2)}) copy-start(f32[20,64]{1,0:T(8,128)} %get-tuple-element.142) | copy-start | bytes 15364
  196.7 4.4 %copy-start.24 = (f32[32,20,16]{0,2,1:T(8,128)S(1)}, f32[32,20,16]{0,2,1:T(8,128)}, u32[]{:S(2)}) copy-start(f32[32,20,16]{0,2,1:T(8,128)} %get-tuple-element.116) | copy-start | bytes 122884
  196.7 4.4 %copy-start.25 = (f32[32,20,16]{0,2,1:T(8,128)S(1)}, f32[32,20,16]{0,2,1:T(8,128)}, u32[]{:S(2)}) copy-start(f32[32,20,16]{0,2,1:T(8,128)} %get-tuple-element.117) | copy-start | bytes 122884
  196.7 4.4 %copy-start.26 = (f32[32,20,16]{0,2,1:T(8,128)S(1)}, f32[32,20,16]{0,2,1:T(8,128)}, u32[]{:S(2)}) copy-start(f32[32,20,16]{0,2,1:T(8,128)} %get-tuple-element.118) | copy-start | bytes 122884
  196.7 4.4 %copy-start.43 = (f32[20,16]{1,0:T(8,128)S(1)}, f32[20,16]{1,0:T(8,128)}, u32[]{:S(2)}) copy-start(f32[20,16]{1,0:T(8,128)} %get-tuple-element.141) | copy-start | bytes 3844
  201.1 8.9 %copy-start.3 = (f32[32,32,64]{1,0,2:T(8,128)S(1)}, f32[32,32,64]{1,0,2:T(8,128)}, u32[]{:S(2)}) copy-start(f32[32,32,64]{1,0,2:T(8,128)} %copy-done.2) | copy-start | bytes 786436
  201.1 8.9 %copy-start.20 = (f32[64,16,32]{2,1,0:T(8,128)S(1)}, f32[64,16,32]{2,1,0:T(8,128)}, u32[]{:S(2)}) copy-start(f32[64,16,32]{2,1,0:T(8,128)} %fusion.130) | copy-start | bytes 393220
  (30 other events, 92.1 us)
Sparse Core Ops, SparseCore 0:
  20.6 72.6 all-gather.1
where the time goes:
time: 222 us; the launch traced here: 221 us
  matrix products  83.1 us (37%)
  local copies, waits for them, and re-layouts  55.7 us (25%)
  blocking collectives  50.4 us (23%)
  between operations  14.5 us (7%)
  starting transfers between devices  10.7 us (5%)
  other arithmetic  6.98 us (3%)
    all_gather x1, blocking collectives, body(): lax.all_gather(stacked_prox, 'leaf', axis=2, tiled=True)  50.4 us
    dot_general x4, matrix products, one_block(): return jnp.einsum('absn,bksn->akn', kernel, coeff_blk, precision=highest)  43.6 us
    dot_general x5, matrix products, near_local(): jnp.einsum('nij,knj->kni', kernel, window[:vectors], precision=highest)  30.2 us
    gather x4, local copies, waits for them, and re-layouts, one_block(): coeff_blk = jnp.take(lookup, clipped_blk, axis=2)  10.6 us
    gather x7, local copies, waits for them, and re-layouts, one_block(): prox_blk = jnp.take(source_prox, clipped_blk, axis=2)  10.4 us
    ppermute x2, starting transfers between devices, with_halo_2(): lax.ppermute(tail, axis, [(i, (i + 1) % count) for i in range(ends)])  8.1 us
    slice x2, local copies, waits for them, and re-layouts, body(): gathered_coeffs[:, :, :, begin_at:begin_at + extent]  5.94 us
    sub x10, local copies, waits for them, and re-layouts, kernel_sq(): left_pts[0] - right_pts[0]  4.64 us
  transfers between devices with their start and end apart: 5, of which 0 were waited for; matrix products, arithmetic and copies ran while one was open for 46% of the time, Pallas kernels for 0%

commit v1 on v0

--- a/solution.py
+++ b/solution.py
@@ -11,6 +11,18 @@
 LEAF_DEV = 64
 kernel_band = 0.1
 highest = lax.Precision.HIGHEST
+
+
+def gather_by_bits(value, axis, dim):
+    ways, here, step = (lax.axis_size(axis), lax.axis_index(axis), value.shape[dim])
+    line, have = (value, 1)
+    while have < ways:
+        line = jnp.concatenate(
+            [line, lax.ppermute(line, axis, [(d, (d - have) % ways) for d in range(ways)])],
+            axis=dim,
+        )
+        have = 2 * have
+    return jnp.roll(line, here * step, axis=dim)
 
 
 def with_halo_2(cells, sides, width):
@@ -112,7 +124,7 @@
     stacked_prox = jnp.concatenate(level_prox[:top_count], axis=2)
     gathered_coeffs, gathered_prox = (
         lax.all_gather(stacked_coeffs, "leaf", axis=2, tiled=True),
-        lax.all_gather(stacked_prox, "leaf", axis=2, tiled=True),
+        gather_by_bits(stacked_prox, "leaf", 2),
     )
     group = stacked_coeffs.shape[2]
     roots = gathered_coeffs.shape[2] // group

time: 222 us -> 195 us (0.88)
  blocking collectives: 50.4 us -> 0 us
  starting transfers between devices: 10.7 us -> 21.8 us
  local copies, waits for them, and re-layouts: 55.7 us -> 65.2 us
    all_gather x1 -> x0, blocking collectives: 50.4 us -> none  [body(): lax.all_gather(stacked_prox, 'leaf', axis=2, tiled=True)]
    ppermute x0 -> x5, starting transfers between devices: none -> 14.9 us  [gather_by_bits(): lax.ppermute(line, axis, [(d, (d - have) % ways) for d in range(ways)])]
    slice x4, local copies, waits for them, and re-layouts: 0.44 us -> 4.81 us  [body(): gathered_prox[:, :, :, begin_at:begin_at + extent]]
    ppermute x2, starting transfers between devices: 8.1 us -> 4.33 us  [with_halo_2(): lax.ppermute(tail, axis, [(i, (i + 1) % count) for i in range(ends)])]
    reshape x3, local copies, waits for them, and re-layouts: 0.69 us -> 3.2 us  [body(): gathered_prox[:, :, :, begin_at:begin_at + extent]]
  transfers between devices with their start and end apart: 5 -> 10, of which waited for: 0 -> 0; matrix products, arithmetic and copies ran while one was open for 46% -> 66% of each run, Pallas kernels for 0% -> 0%
where the time goes in v1:
time: 195 us; the launch traced here: 194 us
  matrix products  83.2 us (43%)
  local copies, waits for them, and re-layouts  65.2 us (33%)
  starting transfers between devices  21.8 us (11%)
  between operations  14.6 us (7%)
  other arithmetic  9.18 us (5%)
    dot_general x4, matrix products, one_block(): return jnp.einsum('absn,bksn->akn', kernel, coeff_blk, precision=highest)  43.6 us
    dot_general x5, matrix products, near_local(): jnp.einsum('nij,knj->kni', kernel, window[:vectors], precision=highest)  30.2 us
    ppermute x5, starting transfers between devices, gather_by_bits(): lax.ppermute(line, axis, [(d, (d - have) % ways) for d in range(ways)])  14.9 us
    gather x7, local copies, waits for them, and re-layouts, one_block(): prox_blk = jnp.take(source_prox, clipped_blk, axis=2)  10.5 us
    gather x4, local copies, waits for them, and re-layouts, one_block(): coeff_blk = jnp.take(lookup, clipped_blk, axis=2)  9.89 us
    slice x2, local copies, waits for them, and re-layouts, body(): gathered_coeffs[:, :, :, begin_at:begin_at + extent]  5.94 us
    slice x4, local copies, waits for them, and re-layouts, body(): gathered_prox[:, :, :, begin_at:begin_at + extent]  4.81 us
    ppermute x2, starting transfers between devices, with_halo_2(): lax.ppermute(tail, axis, [(i, (i + 1) % count) for i in range(ends)])  4.33 us
  transfers between devices with their start and end apart: 10, of which 0 were waited for; matrix products, arithmetic and copies ran while one was open for 66% of the time, Pallas kernels for 0%

profile of v1, /device:TPU:0, one launch (start us, length us, event | category | flops | bytes accessed | tf_op | source)
XLA Modules:
  0.0 194.0 jit_solution(14367985823129712616)
XLA Ops:
  6.5 6.4 %collective-permute-start.4 = (f32[3,32,21]{2,1,0:T(8,128)}, f32[3,32,21]{2,1,0:T(8,128)S(1)}, u32[]{:S(2)}, u32[]{:S(2)}) collective-permute-start(f32[3,32,21]{2,1,0:T(8,128)} %bitcast.203), channel_id=1, source_target_pairs={{0,31},{1,0},{2,1},{3,2},{4,3},{5,4},{6,5},{7,6},{8,7},{9,8},{10,9... | collective-permute-start | bytes 24200 | tf_op jit(solution)/shard_map/ppermute | solution.py:21
  14.2 2.1 %slice.394 = f32[32,32,16]{2,1,0:T(8,128)} slice(f32[32,32,84]{2,1,0:T(8,128)} %param.11), slice={[0:32], [0:32], [4:20]} | slice | bytes 131072 | tf_op jit(solution)/shard_map/slice | solution.py:117
  18.8 1.7 copy.163
  20.8 3.6 %convolution_bitcast_fusion = f32[32,16,64]{0,1,2:T(8,128)S(1)} fusion(f32[32,64,64]{2,1,0:T(8,128)S(1)} %reshape.364, f32[16,64,64]{2,1,0:T(8,128)} %reshape.363), kind=kOutput, calls=%fused_computation.140 | convolution fusion | flops 25165824 | bytes 917504 | tf_op jit(solution)/shard_map/rnp,knp->rkn/dot_general | solution.py:106
  28.2 1.3 collective-permute-start.2
  30.9 3.0 %collective-permute-start = (f32[19,128]{1,0:T(8,128)S(1)}, f32[19,128]{1,0:T(8,128)S(1)}, u32[]{:S(2)}, u32[]{:S(2)}) collective-permute-start(f32[19,128]{1,0:T(8,128)S(1)} %get-tuple-element.119), channel_id=1, source_target_pairs={{0,1},{1,2},{2,3},{3,4},{4,5},{5,6},{6,7},{7,8},{8,9},{9,10},{10,1... | collective-permute-start | bytes 29192 | tf_op jit(solution)/shard_map/ppermute | solution.py:36
  48.6 4.9 %collective-permute-start.5 = (f32[3,32,42]{2,1,0:T(8,128)S(1)}, f32[3,32,42]{2,1,0:T(8,128)S(1)}, u32[]{:S(2)}, u32[]{:S(2)}) collective-permute-start(f32[3,32,42]{2,1,0:T(8,128)S(1)} %pad_maximum_fusion.6), channel_id=1, source_target_pairs={{0,30},{1,31},{2,0},{3,1},{4,2},{5,3},{6,4},{7,5},{8,6},{9,7},{10,... | collective-permute-start | bytes 48392 | tf_op jit(solution)/shard_map/ppermute | solution.py:21
  54.6 6.0 %fusion.87 = f32[64,16,64]{2,1,0:T(8,128)S(1)} fusion(f32[64]{0:T(128)S(1)} %get-tuple-element.145, f32[64,64]{1,0:T(8,128)S(1)} %get-tuple-element.100, f32[64,64]{1,0:T(8,128)S(1)} %get-tuple-element.101, f32[64,64]{1,0:T(8,128)S(1)} %get-tuple-element.102, f32[64,64]{1,0:T(8,128)S(1)} %copy-done.33, f32[64,64]{1,0:T(8,128)S(1)} %copy-done.32, ...), kind=kOutput, calls=%fused_computation.95 | convolution fusion | flops 53215232 | bytes 622848 | tf_op jit(solution)/shard_map/nij,knj->kni/dot_general | solution.py:95
  60.6 6.1 %fusion.74 = f32[64,16,64]{2,1,0:T(8,128)S(1)} fusion(f32[64]{0:T(128)S(1)} %get-tuple-element.144, f32[64,64]{1,0:T(8,128)S(1)} %get-tuple-element.89, f32[64,64]{1,0:T(8,128)S(1)} %get-tuple-element.90, f32[64,64]{1,0:T(8,128)S(1)} %get-tuple-element.98, f32[64,64]{1,0:T(8,128)S(1)} %copy-done.33, f32[64,64]{1,0:T(8,128)S(1)} %copy-done.32, ...), kind=kOutput, calls=%fused_computation.82 | convolution fusion | flops 53215232 | bytes 622848 | tf_op jit(solution)/shard_map/nij,knj->kni/dot_general | solution.py:95
  66.7 6.1 %fusion.48 = f32[64,16,64]{2,1,0:T(8,128)S(1)} fusion(f32[64]{0:T(128)S(1)} %get-tuple-element.147, f32[64,64]{1,0:T(8,128)S(1)} %get-tuple-element.103, f32[64,64]{1,0:T(8,128)S(1)} %get-tuple-element.99, f32[64,64]{1,0:T(8,128)S(1)} %get-tuple-element.88, f32[64,64]{1,0:T(8,128)S(1)} %copy-done.33, f32[64,64]{1,0:T(8,128)S(1)} %copy-done.32, ...), kind=kOutput, calls=%fused_computation.56 | convolution fusion | flops 53215232 | bytes 622848 | tf_op jit(solution)/shard_map/nij,knj->kni/dot_general | solution.py:95
  72.7 6.1 %fusion.138 = f32[64,16,64]{2,1,0:T(8,128)S(1)} fusion(f32[64,16,64]{2,1,0:T(8,128)S(1)} %fusion.74, f32[64,16,64]{2,1,0:T(8,128)S(1)} %fusion.87, f32[64]{0:T(128)S(1)} %get-tuple-element.146, f32[64,64]{1,0:T(8,128)S(1)} %get-tuple-element.104, f32[64,64]{1,0:T(8,128)S(1)} %copy-done.33, f32[64,64]{1,0:T(8,128)S(1)} %get-tuple-element.112, ...), kind=kOutput, calls=%fused_computation.143 | convolution fusion | flops 53346304 | bytes 1147136 | tf_op jit(solution)/shard_map/nij,knj->kni/dot_general | solution.py:95
  78.9 6.0 %fusion.144 = f32[64,16,64]{2,1,0:T(8,128)} fusion(f32[64,16,64]{2,1,0:T(8,128)S(1)} %fusion.48, f32[64,16,64]{2,1,0:T(8,128)S(1)} %fusion.138, f32[64]{0:T(128)S(1)} %get-tuple-element.143, f32[64,64]{1,0:T(8,128)S(1)} %get-tuple-element.86, f32[64,64]{1,0:T(8,128)S(1)} %get-tuple-element.87, f32[64,64]{1,0:T(8,128)S(1)} %get-tuple-element.85, ...), kind=kOutput, calls=%fused_computation.145 | convolution fusion | flops 53346304 | bytes 1147136 | tf_op jit(solution)/shard_map/nij,knj->kni/dot_general | solution.py:95
  85.6 1.7 collective-permute-start.6
  88.1 4.3 %gather_fusion.1 = f32[1280,3,32]{2,1,0:T(4,128)S(1)} fusion(f32[3,32,86]{1,0,2:T(4,128)S(1)} %copy.122, s32[2048]{0:T(1024)S(1)} %pad_clamp_fusion), kind=kCustom, calls=%fused_computation.1 | custom fusion | bytes 988160 | tf_op jit(solution)/shard_map/while/body/eval_jaxpr/jit(_take)/gather | solution.py:70
  92.5 2.5 %copy.152 = f32[20,64,3,32]{1,0,3,2:T(8,128)} copy(f32[20,64,3,32]{3,2,1,0:T(4,128)S(1)} %bitcast.210) | data formatting | bytes 983040 | tf_op jit(solution)/shard_map/while/body/eval_jaxpr/jit(_take)/gather | solution.py:70
  95.0 1.4 select_bitcast_fusion
  99.9 1.8 collective-permute-start.7
  102.4 5.5 %gather_fusion = f32[1280,32,16]{1,2,0:T(8,128)} fusion(f32[32,16,86]{0,1,2:T(8,128)S(1)} %copy.120, s32[2048]{0:T(1024)S(1)} %pad_clamp_fusion), kind=kCustom, calls=%fused_computation | custom fusion | bytes 5248000 | tf_op jit(solution)/shard_map/while/body/eval_jaxpr/jit(_take)/gather | solution.py:69
  109.0 31.4 %fusion.130 = f32[64,16,32]{2,1,0:T(8,128)} fusion(f32[20,64]{1,0:T(8,128)S(1)} %copy-done.41, f32[32,20,64]{0,2,1:T(8,128)} %copy.128, f32[32,64]{0,1:T(8,128)S(1)} %copy-done.30, f32[32,20,64]{0,2,1:T(8,128)S(1)} %copy-done.15, f32[32,64]{0,1:T(8,128)S(1)} %copy-done.29, f32[32,20,64]{0,2,1:T(8,128)S(1)} %copy.124, f32[32,64]{0,1:T(8,128)S(1)} %copy-done.28, ...), kind=kOutput, calls=%fused_computation.141 | convolution fusion | flops 266731520 | bytes 3275008 | tf_op jit(solution)/shard_map/while/body/eval_jaxpr/absn,bksn->akn/dot_general | solution.py:74
  141.8 1.9 reshape.373
  144.1 1.7 slice.467
  147.6 1.4 copy.156
  149.0 1.7 copy.136
  150.7 1.7 copy.137
  152.4 2.2 %gather_fusion.3 = f32[320,3,32]{2,1,0:T(4,128)S(1)} fusion(f32[3,32,512]{1,0,2:T(4,128)S(1)} %copy.137, s32[1024]{0:T(1024)S(1)} %copy-done.22), kind=kCustom, calls=%fused_computation.3 | custom fusion | bytes 247040 | tf_op jit(solution)/shard_map/while/body/eval_jaxpr/jit(_take)/gather | solution.py:70
  157.9 1.3 slice.471
  160.2 4.6 %slice.466 = f32[32,16,32,16]{0,1,3,2:T(8,128)} slice(f32[32,16,32,21]{0,1,3,2:T(8,128)} %bitcast.213), slice={[0:32], [0:16], [0:32], [5:21]} | slice | bytes 2097152 | tf_op jit(solution)/shard_map/slice | solution.py:138
  166.2 3.0 %gather_fusion.2 = f32[320,32,16]{1,2,0:T(8,128)S(1)} fusion(f32[32,16,512]{0,1,2:T(8,128)} %bitcast.200, s32[1024]{0:T(1024)S(1)} %copy-done.22), kind=kCustom, calls=%fused_computation.2 | custom fusion | bytes 1312000 | tf_op jit(solution)/shard_map/while/body/eval_jaxpr/jit(_take)/gather | solution.py:69
  169.4 3.2 %fusion.153 = f32[4,16,32]{2,1,0:T(8,128)S(1)} fusion(f32[20,4,32,16]{2,3,1,0:T(8,128)S(1)} %bitcast.198, f32[20,4]{1,0:T(8,128)} %get-tuple-element.139, f32[32,20,4]{0,2,1:T(4,128)} %get-tuple-element.124, f32[32,4]{0,1:T(4,128)} %bitcast.236, f32[32,20,4]{0,2,1:T(4,128)} %get-tuple-element.125, f32[32,4]{0,1:T(4,128)} %bitcast.235, ...), kind=kOutput, calls=%fused_computation.150 | convolution fusion | flops 16670720 | bytes 204688 | tf_op jit(solution)/shard_map/while/body/eval_jaxpr/absn,bksn->akn/dot_general | solution.py:74
  173.8 8.3 %fusion.148 = f32[16,16,32]{2,1,0:T(8,128)S(1)} fusion(f32[20,16]{1,0:T(8,128)S(1)} %copy-done.40, f32[32,20,16]{0,2,1:T(8,128)S(1)} %copy-done.26, f32[32,16]{0,1:T(8,128)S(1)} %copy-done.44, f32[32,20,16]{0,2,1:T(8,128)S(1)} %copy-done.27, f32[32,16]{0,1:T(8,128)S(1)} %copy-done.43, f32[32,20,16]{0,2,1:T(8,128)S(1)} %copy-done.25, ...), kind=kOutput, calls=%fused_computation.149 | convolution fusion | flops 66682880 | bytes 818752 | tf_op jit(solution)/shard_map/while/body/eval_jaxpr/absn,bksn->akn/dot_general | solution.py:74
  182.7 1.7 fusion.129
  184.5 1.6 fusion.128
  (211 shorter events, 43.4 us)
Async XLA Ops:
  6.5 9.7 %copy-start.18 = (f32[32,4096]{1,0:T(8,128)S(1)}, f32[32,4096]{1,0:T(8,128)}, u32[]{:S(2)}) copy-start(f32[32,4096]{1,0:T(8,128)} %param.10) | copy-start | bytes 1572868
  6.5 10.1 %copy-start.11 = (f32[16,4096]{1,0:T(8,128)S(1)}, f32[16,4096]{1,0:T(8,128)}, u32[]{:S(2)}) copy-start(f32[16,4096]{1,0:T(8,128)} %param.9) | copy-start | bytes 786436
  6.5 151.3 %all-gather.2.cloned.1.call-start = ((), (), s32[]{:S(2)}) async-start(), calls=%async_computation | async-start | bytes 5677056 | tf_op jit(solution)/shard_map/all_gather | solution.py:126
  6.5 41.9 %collective-permute-start.4 = (f32[3,32,21]{2,1,0:T(8,128)}, f32[3,32,21]{2,1,0:T(8,128)S(1)}, u32[]{:S(2)}, u32[]{:S(2)}) collective-permute-start(f32[3,32,21]{2,1,0:T(8,128)} %bitcast.203), channel_id=1, source_target_pairs={{0,31},{1,0},{2,1},{3,2},{4,3},{5,4},{6,5},{7,6},{8,7},{9,8},{10,9... | collective-permute-start | bytes 24200 | tf_op jit(solution)/shard_map/ppermute | solution.py:21
  16.7 7.7 %copy-start = (f32[32,64,64]{2,1,0:T(8,128)}, f32[32,64,64]{2,1,0:T(8,128)S(1)}, u32[]{:S(2)}) copy-start(f32[32,64,64]{2,1,0:T(8,128)S(1)} %reshape.364) | copy-start | bytes 1572868
  18.8 6.7 %copy-start.2 = (f32[32,32,64]{1,0,2:T(8,128)}, f32[32,32,64]{1,0,2:T(8,128)S(1)}, u32[]{:S(2)}) copy-start(f32[32,32,64]{1,0,2:T(8,128)S(1)} %copy.162) | copy-start | bytes 786436
  20.5 5.0 %copy-start.7 = (f32[32,32,16]{1,0,2:T(8,128)}, f32[32,32,16]{1,0,2:T(8,128)S(1)}, u32[]{:S(2)}) copy-start(f32[32,32,16]{1,0,2:T(8,128)S(1)} %copy.163) | copy-start | bytes 196612
  20.8 5.1 %copy-start.16 = (f32[32,32,4]{1,0,2:T(8,128)}, f32[32,32,4]{1,0,2:T(8,128)S(1)}, u32[]{:S(2)}) copy-start(f32[32,32,4]{1,0,2:T(8,128)S(1)} %copy.164) | copy-start | bytes 49156
  25.5 5.3 %copy-start.12 = (f32[16,4096]{1,0:T(8,128)S(1)}, f32[16,4096]{1,0:T(8,128)}, u32[]{:S(2)}) copy-start(f32[16,4096]{1,0:T(8,128)} %param.9) | copy-start | bytes 786436
  25.5 5.3 %copy-start.24 = (f32[3,4096]{1,0:T(4,128)S(1)}, f32[3,4096]{1,0:T(4,128)}, u32[]{:S(2)}) copy-start(f32[3,4096]{1,0:T(4,128)} %param.8) | copy-start | bytes 147460
  25.5 9.7 %copy-start.21 = (s32[84,20]{0,1:T(8,128)S(1)}, s32[84,20]{0,1:T(8,128)}, u32[]{:S(2)}) copy-start(s32[84,20]{0,1:T(8,128)} %param.14) | copy-start | bytes 20164
  25.5 10.5 %copy-start.52 = (s32[1,32]{1,0:T(1,128)S(1)}, s32[1,32]{1,0:T(1,128)}, u32[]{:S(2)}) copy-start(s32[1,32]{1,0:T(1,128)} %param.15) | copy-start | bytes 388
  25.5 13.7 %copy-start.46 = (s32[64,5]{0,1:T(8,128)S(1)}, s32[64,5]{0,1:T(8,128)}, u32[]{:S(2)}) copy-start(s32[64,5]{0,1:T(8,128)} %param.13) | copy-start | bytes 3844
  27.3 60.0 %copy-start.13 = (f32[3,32,64]{2,1,0:T(8,128)}, f32[3,32,64]{2,1,0:T(8,128)S(1)}, u32[]{:S(2)}) copy-start(f32[3,32,64]{2,1,0:T(8,128)S(1)} %slice.381) | copy-start | bytes 73732
  28.2 59.0 %collective-permute-start.2 = (f32[608,11]{1,0:T(8,128)}, f32[608,11]{1,0:T(8,128)S(1)}, u32[]{:S(2)}, u32[]{:S(2)}) collective-permute-start(f32[608,11]{1,0:T(8,128)} %get-tuple-element.121), channel_id=1, source_target_pairs={{0,1},{1,2},{2,3},{3,4},{4,5},{5,6},{6,7},{7,8},{8,9},{9,10},{10,1... | collective-permute-start | bytes 80264 | tf_op jit(solution)/shard_map/ppermute | solution.py:36
  29.5 57.7 %collective-permute-start.3 = (f32[608,11]{1,0:T(8,128)}, f32[608,11]{1,0:T(8,128)S(1)}, u32[]{:S(2)}, u32[]{:S(2)}) collective-permute-start(f32[608,11]{1,0:T(8,128)} %get-tuple-element.122), channel_id=1, source_target_pairs={{1,0},{2,1},{3,2},{4,3},{5,4},{6,5},{7,6},{8,7},{9,8},{10,9},{11,1... | collective-permute-start | bytes 80264 | tf_op jit(solution)/shard_map/ppermute | solution.py:38
  30.9 22.6 %collective-permute-start = (f32[19,128]{1,0:T(8,128)S(1)}, f32[19,128]{1,0:T(8,128)S(1)}, u32[]{:S(2)}, u32[]{:S(2)}) collective-permute-start(f32[19,128]{1,0:T(8,128)S(1)} %get-tuple-element.119), channel_id=1, source_target_pairs={{0,1},{1,2},{2,3},{3,4},{4,5},{5,6},{6,7},{7,8},{8,9},{9,10},{10,1... | collective-permute-start | bytes 29192 | tf_op jit(solution)/shard_map/ppermute | solution.py:36
  33.9 19.5 %collective-permute-start.1 = (f32[19,128]{1,0:T(8,128)S(1)}, f32[19,128]{1,0:T(8,128)S(1)}, u32[]{:S(2)}, u32[]{:S(2)}) collective-permute-start(f32[19,128]{1,0:T(8,128)S(1)} %get-tuple-element.120), channel_id=1, source_target_pairs={{1,0},{2,1},{3,2},{4,3},{5,4},{6,5},{7,6},{8,7},{9,8},{10,9},{11,1... | collective-permute-start | bytes 29192 | tf_op jit(solution)/shard_map/ppermute | solution.py:38
  48.6 36.3 %collective-permute-start.5 = (f32[3,32,42]{2,1,0:T(8,128)S(1)}, f32[3,32,42]{2,1,0:T(8,128)S(1)}, u32[]{:S(2)}, u32[]{:S(2)}) collective-permute-start(f32[3,32,42]{2,1,0:T(8,128)S(1)} %pad_maximum_fusion.6), channel_id=1, source_target_pairs={{0,30},{1,31},{2,0},{3,1},{4,2},{5,3},{6,4},{7,5},{8,6},{9,7},{10,... | collective-permute-start | bytes 48392 | tf_op jit(solution)/shard_map/ppermute | solution.py:21
  85.6 13.4 %collective-permute-start.6 = (f32[3,32,84]{2,1,0:T(8,128)}, f32[3,32,84]{2,1,0:T(8,128)}, u32[]{:S(2)}, u32[]{:S(2)}) collective-permute-start(f32[3,32,84]{2,1,0:T(8,128)} %pad_maximum_fusion.7), channel_id=1, source_target_pairs={{0,28},{1,29},{2,30},{3,31},{4,0},{5,1},{6,2},{7,3},{8,4},{9,5},{1... | collective-permute-start | bytes 96776 | tf_op jit(solution)/shard_map/ppermute | solution.py:21
  96.5 5.2 %copy-start.10 = (f32[608,11]{1,0:T(8,128)S(1)}, f32[608,11]{1,0:T(8,128)}, u32[]{:S(2)}) copy-start(f32[608,11]{1,0:T(8,128)} %copy-done.9) | copy-start | bytes 80260
  96.5 5.2 %copy-start.14 = (f32[3,32,64]{2,1,0:T(8,128)S(1)}, f32[3,32,64]{2,1,0:T(8,128)}, u32[]{:S(2)}) copy-start(f32[3,32,64]{2,1,0:T(8,128)} %copy-done.13) | copy-start | bytes 73732
  99.9 8.0 %collective-permute-start.7 = (f32[3,32,168]{2,1,0:T(8,128)S(1)}, f32[3,32,168]{2,1,0:T(8,128)S(1)}, u32[]{:S(2)}, u32[]{:S(2)}) collective-permute-start(f32[3,32,168]{2,1,0:T(8,128)S(1)} %pad_maximum_fusion.4), channel_id=1, source_target_pairs={{0,24},{1,25},{2,26},{3,27},{4,28},{5,29},{6,30},{7,31},{8,0},{9,1... | collective-permute-start | bytes 193544 | tf_op jit(solution)/shard_map/ppermute | solution.py:21
  102.4 6.6 %copy-start.15 = (f32[32,20,64]{0,2,1:T(8,128)S(1)}, f32[32,20,64]{0,2,1:T(8,128)}, u32[]{:S(2)}) copy-start(f32[32,20,64]{0,2,1:T(8,128)} %copy.126) | copy-start | bytes 491524
  102.4 6.6 %copy-start.28 = (f32[32,64]{0,1:T(8,128)S(1)}, f32[32,64]{0,1:T(8,128)}, u32[]{:S(2)}) copy-start(f32[32,64]{0,1:T(8,128)} %copy.121) | copy-start | bytes 24580
  102.4 6.6 %copy-start.29 = (f32[32,64]{0,1:T(8,128)S(1)}, f32[32,64]{0,1:T(8,128)}, u32[]{:S(2)}) copy-start(f32[32,64]{0,1:T(8,128)} %copy.125) | copy-start | bytes 24580
  102.4 6.6 %copy-start.30 = (f32[32,64]{0,1:T(8,128)S(1)}, f32[32,64]{0,1:T(8,128)}, u32[]{:S(2)}) copy-start(f32[32,64]{0,1:T(8,128)} %copy.127) | copy-start | bytes 24580
  102.4 6.6 %copy-start.41 = (f32[20,64]{1,0:T(8,128)S(1)}, f32[20,64]{1,0:T(8,128)}, u32[]{:S(2)}) copy-start(f32[20,64]{1,0:T(8,128)} %get-tuple-element.142) | copy-start | bytes 15364
  108.9 31.5 %collective-permute-start.8 = (f32[3,32,336]{2,1,0:T(8,128)S(1)}, f32[3,32,336]{2,1,0:T(8,128)S(1)}, u32[]{:S(2)}, u32[]{:S(2)}) collective-permute-start(f32[3,32,336]{2,1,0:T(8,128)S(1)} %concatenate.53), channel_id=1, source_target_pairs={{0,16},{1,17},{2,18},{3,19},{4,20},{5,21},{6,22},{7,23},{8,24},{9,... | collective-permute-start | bytes 387080 | tf_op jit(solution)/shard_map/ppermute | solution.py:21
  173.7 8.4 %copy-start.8 = (f32[32,32,16]{1,0,2:T(8,128)S(1)}, f32[32,32,16]{1,0,2:T(8,128)}, u32[]{:S(2)}) copy-start(f32[32,32,16]{1,0,2:T(8,128)} %copy-done.7) | copy-start | bytes 196612
  173.8 8.9 %copy-start.3 = (f32[32,32,64]{1,0,2:T(8,128)S(1)}, f32[32,32,64]{1,0,2:T(8,128)}, u32[]{:S(2)}) copy-start(f32[32,32,64]{1,0,2:T(8,128)} %copy-done.2) | copy-start | bytes 786436
  173.8 8.9 %copy-start.20 = (f32[64,16,32]{2,1,0:T(8,128)S(1)}, f32[64,16,32]{2,1,0:T(8,128)}, u32[]{:S(2)}) copy-start(f32[64,16,32]{2,1,0:T(8,128)} %fusion.130) | copy-start | bytes 393220
  (32 other events, 100.7 us)
Sparse Core Ops, SparseCore 0:
  27.0 65.0 all-gather.1
